TPU v7x, 32 devices: a whole 2x2x4 slice. The times are simulated.
32 devices in a mesh: blk: 8 (over y, x, core), uly: 4 (over z).
Axes of the slice: x: 2, y: 2, z: 4, core: 2. Of those that a mesh axis runs over, the one named last changes fastest.
Arguments:
- tokens: bfloat16 [4096, 2048], P(('blk', 'uly')), may hold values from -6 to 6
- doc_starts: int32 [16], replicated, may hold values from 0 to 4095, as said below
- attn_gain: bfloat16 [2048], P(('blk', 'uly')), may hold values from 0.25 to 1.75
- qk_gains: bfloat16 [128], P(('blk', 'uly')), may hold values from 0.25 to 1.75
- q_weight: bfloat16 [2048, 2048], P(('blk', 'uly')), may hold values from -0.125 to 0.125
- k_weight: bfloat16 [512, 2048], P(('blk', 'uly')), may hold values from -0.125 to 0.125
- v_weight: bfloat16 [512, 2048], P(('blk', 'uly')), may hold values from -0.125 to 0.125
- out_weight: bfloat16 [2048, 2048], P(('blk', 'uly')), may hold values from -1 to 1
- ffn_gain: bfloat16 [2048], P(('blk', 'uly')), may hold values from 0.25 to 1.75
- gate_weight: bfloat16 [8192, 2048], P(('blk', 'uly')), may hold values from -0.125 to 0.125
- up_weight: bfloat16 [8192, 2048], P(('blk', 'uly')), may hold values from -0.125 to 0.125
- down_weight: bfloat16 [8192, 2048], P(('blk', 'uly')), may hold values from -0.0625 to 0.0625
- out_grad: bfloat16 [4096, 2048], P(('blk', 'uly')), may hold values from -6 to 6
Outputs:
- output: float32 [4096, 2048], P(('blk', 'uly'))
- input_grad: float32 [4096, 2048], P(('blk', 'uly'))
- attn_gain_grad: float32 [2048], P(('blk', 'uly'))
- qk_gains_grad: float32 [128], P(('blk', 'uly'))
- q_weight_grad: float32 [2048, 2048], P(('blk', 'uly'))
- k_weight_grad: float32 [512, 2048], P(('blk', 'uly'))
- v_weight_grad: float32 [512, 2048], P(('blk', 'uly'))
- out_weight_grad: float32 [2048, 2048], P(('blk', 'uly'))
- ffn_gain_grad: float32 [2048], P(('blk', 'uly'))
- gate_weight_grad: float32 [8192, 2048], P(('blk', 'uly'))
- up_weight_grad: float32 [8192, 2048], P(('blk', 'uly'))
- down_weight_grad: float32 [8192, 2048], P(('blk', 'uly'))
Inputs may be any that keep to these rules, and one draw needn't show every extreme that they name: doc_starts[0] = 0 and the starts rise strictly; a document runs from its start to the next start, the last one to 4096; every document holds at most 2048 tokens, and one holds exactly 2048.
All inputs are finite; a program needn't handle non-finite values.
Results may differ from a plain program's by a relative error of at most 0.03.
Values may be sent and summed in bfloat16 or wider, within the bound.
A program may use at most 256 MiB of HBM per device.

v0:
```python
import jax
import jax.numpy as jnp
from jax import lax
from jax.sharding import PartitionSpec as P

H = 32
KVH = 8
HD = 64
DOC_MAX = 2048


NORM_EPSILON = 1e-05
ROPE_THETA = 1000000.0
MASKED_SCORE = -1e30


def shifted(value, axis, by):
    peers = lax.axis_size(axis)
    pairs = [(i, i + by) for i in range(peers) if 0 <= i + by < peers]
    return lax.ppermute(value, axis, pairs)


def for_sending(value):
    return jax.tree.map(lambda a: a.astype(jnp.bfloat16) if a.dtype == jnp.float32 else a, value)


def rms_forward(values, gain):
    inverse = lax.rsqrt(jnp.mean(values * values, axis=-1, keepdims=True) + NORM_EPSILON)
    return (values * inverse * gain, inverse)


def rms_backward(values, inverse, gain, upstream):
    scaled = upstream * gain
    gain_grad = jnp.sum((upstream * values * inverse).reshape(-1, values.shape[-1]), axis=0)
    values_grad = inverse * scaled - values * inverse**3 * jnp.mean(
        scaled * values, axis=-1, keepdims=True
    )
    return (values_grad, gain_grad)


def rotate(values, cosine, sine):
    half_width = values.shape[-1] // 2
    front_half = values[..., :half_width]
    back_half = values[..., half_width:]
    return jnp.concatenate(
        [front_half * cosine - back_half * sine, back_half * cosine + front_half * sine], axis=-1
    )


def project(inputs, weight):
    return lax.dot_general(
        inputs, weight, (((1,), (1,)), ((), ())), preferred_element_type=jnp.float32
    )


def weight_grad(upstream, inputs):
    return lax.dot_general(
        upstream, inputs, (((0,), (0,)), ((), ())), preferred_element_type=jnp.float32
    )


def spread_back(upstream, weight):
    return jnp.dot(upstream, weight, preferred_element_type=jnp.float32)


def doc_start_of(row_ids, doc_starts):
    return jnp.max(
        jnp.where(doc_starts[None, :] <= row_ids[:, None], doc_starts[None, :], 0), axis=1
    )


def on_device(
    tokens,
    doc_starts,
    attn_gain,
    qk_gains,
    q_weight,
    k_weight,
    v_weight,
    out_weight,
    ffn_gain,
    gate_weight,
    up_weight,
    down_weight,
    out_grad,
):
    blk_count = lax.axis_size("blk")
    uly_count = lax.axis_size("uly")
    blk_index = lax.axis_index("blk")
    uly_index = lax.axis_index("uly")
    tok_rows = tokens.shape[0]
    span_rows = tok_rows * uly_count
    total_rows = span_rows * blk_count
    longest = min(DOC_MAX, total_rows // 2)
    reach_blocks = min((longest + span_rows - 2) // span_rows, blk_count - 1)
    kv_local = KVH // uly_count
    group_size = H // KVH
    kv_width = kv_local * HD
    score_scale = HD ** (-0.5)
    q_full, k_full, v_full, o_full, attn_gain_full, ffn_gain_full, qk_full = (
        lax.all_gather(q_weight, ("blk", "uly"), axis=0, tiled=True),
        lax.all_gather(k_weight, ("blk", "uly"), axis=0, tiled=True),
        lax.all_gather(v_weight, ("blk", "uly"), axis=0, tiled=True),
        lax.all_gather(out_weight, ("blk", "uly"), axis=0, tiled=True),
        lax.all_gather(attn_gain, ("blk", "uly"), axis=0, tiled=True),
        lax.all_gather(ffn_gain, ("blk", "uly"), axis=0, tiled=True),
        lax.all_gather(qk_gains, ("blk", "uly"), axis=0, tiled=True),
    )
    attn_gain_f = attn_gain_full.astype(jnp.float32)
    ffn_gain_f = ffn_gain_full.astype(jnp.float32)
    q_gain = qk_full[:HD].astype(jnp.float32)
    k_gain = qk_full[HD:].astype(jnp.float32)
    own_rows = (blk_index * uly_count + uly_index) * tok_rows + jnp.arange(
        tok_rows, dtype=jnp.int32
    )
    positions = (own_rows - doc_start_of(own_rows, doc_starts)).astype(jnp.float32)
    frequency = ROPE_THETA ** (-jnp.arange(HD // 2, dtype=jnp.float32) * 2.0 / HD)
    angle = positions[:, None] * frequency[None, :]
    cosine = jnp.cos(angle)[:, None, :]
    sine = jnp.sin(angle)[:, None, :]
    hidden_in = tokens.astype(jnp.float32)
    normed_one, inverse_one = rms_forward(hidden_in, attn_gain_f)
    normed_low = normed_one.astype(jnp.bfloat16)
    q_raw = project(normed_low, q_full)
    k_raw = project(normed_low, k_full)
    v_raw = project(normed_low, v_full)
    q_heads = q_raw.reshape(tok_rows, H, HD)
    k_heads = k_raw.reshape(tok_rows, KVH, HD)
    q_normed, q_inverse = rms_forward(q_heads, q_gain)
    k_normed, k_inverse = rms_forward(k_heads, k_gain)
    q_low = rotate(q_normed, cosine, sine).reshape(tok_rows, H * HD).astype(jnp.bfloat16)
    k_low = rotate(k_normed, cosine, sine).reshape(tok_rows, KVH * HD).astype(jnp.bfloat16)
    v_low = v_raw.astype(jnp.bfloat16)
    q_seq, k_seq, v_seq = (
        lax.all_to_all(q_low, "uly", split_axis=1, concat_axis=0, tiled=True),
        lax.all_to_all(k_low, "uly", split_axis=1, concat_axis=0, tiled=True),
        lax.all_to_all(v_low, "uly", split_axis=1, concat_axis=0, tiled=True),
    )
    kv_own = jnp.concatenate([k_seq, v_seq], axis=1)
    near_blocks = [kv_own]
    for offset in range(1, reach_blocks + 1):
        near_blocks.append(shifted(kv_own, "blk", offset))
    kv_stack = jnp.stack(near_blocks)
    block_ids = jnp.arange(reach_blocks + 1, dtype=jnp.int32)
    span_start = blk_index * span_rows
    row_offsets = jnp.arange(span_rows, dtype=jnp.int32)
    query_rows = span_start + row_offsets
    query_doc = doc_start_of(query_rows, doc_starts)
    queries = q_seq.reshape(span_rows, kv_local, group_size, HD)

    def block_live(block_id):
        return span_start - block_id * span_rows + span_rows - 1 >= query_doc[0]

    def block_scores(kv_block, block_id):
        key_rows = span_start - block_id * span_rows + row_offsets
        key_heads = kv_block[:, :kv_width].reshape(span_rows, kv_local, HD)
        value_heads = kv_block[:, kv_width:].reshape(span_rows, kv_local, HD)
        raw_scores = (
            jnp.einsum("qkgd,skd->qkgs", queries, key_heads, preferred_element_type=jnp.float32)
            * score_scale
        )
        allowed = (key_rows[None, :] >= query_doc[:, None]) & (
            key_rows[None, :] <= query_rows[:, None]
        )
        return (
            jnp.where(allowed[:, None, None, :], raw_scores, MASKED_SCORE),
            key_heads,
            value_heads,
        )

    def forward_block(carry, block_input):
        kv_block, block_id = block_input

        def live_update(state):
            running_top, running_total, running_sum = state
            scores, key_heads, value_heads = block_scores(kv_block, block_id)
            new_top = jnp.maximum(running_top, jnp.max(scores, axis=-1))
            factor = jnp.exp(running_top - new_top)
            unscaled = jnp.exp(scores - new_top[..., None])
            new_total = running_total * factor + jnp.sum(unscaled, axis=-1)
            new_sum = running_sum * factor[..., None] + jnp.einsum(
                "qkgs,skd->qkgd",
                unscaled.astype(jnp.bfloat16),
                value_heads,
                preferred_element_type=jnp.float32,
            )
            return (new_top, new_total, new_sum)

        def skip_update(state):
            return state

        return (lax.cond(block_live(block_id), live_update, skip_update, carry), None)

    start_state = (
        jnp.full((span_rows, kv_local, group_size), MASKED_SCORE, jnp.float32),
        jnp.zeros((span_rows, kv_local, group_size), jnp.float32),
        jnp.zeros((span_rows, kv_local, group_size, HD), jnp.float32),
    )
    (running_top, running_total, running_sum), _ = lax.scan(
        forward_block, start_state, (kv_stack, block_ids)
    )
    attn_f32 = running_sum / running_total[..., None]
    log_total = running_top + jnp.log(running_total)
    attn_low = attn_f32.reshape(span_rows, kv_width * group_size).astype(jnp.bfloat16)
    attn_tok = lax.all_to_all(attn_low, "uly", split_axis=0, concat_axis=1, tiled=True)
    hidden = hidden_in + project(attn_tok, o_full)
    normed_two, inverse_two = rms_forward(hidden, ffn_gain_f)
    normed_two_low = normed_two.astype(jnp.bfloat16)
    normed_seq, grad_seq = (
        lax.all_gather(normed_two_low, "uly", axis=0, tiled=True),
        lax.all_gather(out_grad, "uly", axis=0, tiled=True),
    )
    gate_part, up_part, down_part = (
        lax.all_gather(gate_weight, "blk", axis=0, tiled=True),
        lax.all_gather(up_weight, "blk", axis=0, tiled=True),
        lax.all_gather(down_weight, "blk", axis=0, tiled=True),
    )
    gate = project(normed_seq, gate_part)
    upward = project(normed_seq, up_part)
    sigmoid_gate = jax.nn.sigmoid(gate)
    silu_gate = gate * sigmoid_gate
    active_low = (silu_gate * upward).astype(jnp.bfloat16)
    mlp_term = spread_back(active_low, down_part)
    mlp_out = lax.psum_scatter(
        mlp_term.astype(jnp.bfloat16), "uly", scatter_dimension=0, tiled=True
    ).astype(jnp.float32)
    output = hidden + mlp_out
    gate_back, up_back, down_back = (
        lax.all_gather(gate_weight, "blk", axis=0, tiled=True),
        lax.all_gather(up_weight, "blk", axis=0, tiled=True),
        lax.all_gather(down_weight, "blk", axis=0, tiled=True),
    )
    down_wgrad = weight_grad(active_low, grad_seq)
    active_grad = project(grad_seq, down_back)
    silu_slope = sigmoid_gate * (1.0 + gate * (1.0 - sigmoid_gate))
    gate_grad = (active_grad * upward * silu_slope).astype(jnp.bfloat16)
    up_grad = (active_grad * silu_gate).astype(jnp.bfloat16)
    gate_wgrad = weight_grad(gate_grad, normed_seq)
    up_wgrad = weight_grad(up_grad, normed_seq)
    normed_term = spread_back(gate_grad, gate_back) + spread_back(up_grad, up_back)
    normed_two_grad = lax.psum_scatter(
        normed_term.astype(jnp.bfloat16), "uly", scatter_dimension=0, tiled=True
    ).astype(jnp.float32)
    hidden_norm_grad, ffn_gain_grad = rms_backward(hidden, inverse_two, ffn_gain_f, normed_two_grad)
    hidden_grad = out_grad.astype(jnp.float32) + hidden_norm_grad
    hidden_low = hidden_grad.astype(jnp.bfloat16)
    out_wgrad = weight_grad(hidden_low, attn_tok)
    attn_grad_low = spread_back(hidden_low, o_full).astype(jnp.bfloat16)
    grad_seq_heads = lax.all_to_all(attn_grad_low, "uly", split_axis=1, concat_axis=0, tiled=True)
    grad_heads = grad_seq_heads.reshape(span_rows, kv_local, group_size, HD)
    delta = jnp.sum(grad_heads.astype(jnp.float32) * attn_f32, axis=-1)

    def backward_block(q_grad, block_input):
        kv_block, block_id = block_input

        def live_grad(q_grad_in):
            scores, key_heads, value_heads = block_scores(kv_block, block_id)
            probs = jnp.exp(scores - log_total[..., None])
            prob_grad = jnp.einsum(
                "qkgd,skd->qkgs", grad_heads, value_heads, preferred_element_type=jnp.float32
            )
            score_grad = (probs * (prob_grad - delta[..., None])).astype(jnp.bfloat16)
            q_grad_out = (
                q_grad_in
                + jnp.einsum(
                    "qkgs,skd->qkgd", score_grad, key_heads, preferred_element_type=jnp.float32
                )
                * score_scale
            )
            key_grad = (
                jnp.einsum(
                    "qkgs,qkgd->skd", score_grad, queries, preferred_element_type=jnp.float32
                )
                * score_scale
            )
            value_grad = jnp.einsum(
                "qkgs,qkgd->skd",
                probs.astype(jnp.bfloat16),
                grad_heads,
                preferred_element_type=jnp.float32,
            )
            return (
                q_grad_out,
                jnp.concatenate(
                    [
                        key_grad.reshape(span_rows, kv_width),
                        value_grad.reshape(span_rows, kv_width),
                    ],
                    axis=1,
                ),
            )

        def skip_grad(q_grad_in):
            return (q_grad_in, jnp.zeros((span_rows, 2 * kv_width), jnp.float32))

        return lax.cond(block_live(block_id), live_grad, skip_grad, q_grad)

    q_grad_seq, kv_grads = lax.scan(
        backward_block,
        jnp.zeros((span_rows, kv_local, group_size, HD), jnp.float32),
        (kv_stack, block_ids),
    )
    kv_total = kv_grads[0]
    for offset in range(1, reach_blocks + 1):
        kv_total = kv_total + shifted(kv_grads[offset].astype(jnp.bfloat16), "blk", -offset).astype(
            jnp.float32
        )
    q_grad_tok, k_grad_tok, v_grad_tok = (
        lax.all_to_all(
            q_grad_seq.reshape(span_rows, kv_width * group_size).astype(jnp.bfloat16),
            "uly",
            split_axis=0,
            concat_axis=1,
            tiled=True,
        ).astype(jnp.float32),
        lax.all_to_all(
            for_sending(kv_total[:, :kv_width]), "uly", split_axis=0, concat_axis=1, tiled=True
        ),
        lax.all_to_all(
            for_sending(kv_total[:, kv_width:]), "uly", split_axis=0, concat_axis=1, tiled=True
        ),
    )
    q_turned = rotate(q_grad_tok.reshape(tok_rows, H, HD), cosine, -sine)
    k_turned = rotate(k_grad_tok.reshape(tok_rows, KVH, HD), cosine, -sine)
    q_raw_grad, q_gain_grad = rms_backward(q_heads, q_inverse, q_gain, q_turned)
    k_raw_grad, k_gain_grad = rms_backward(k_heads, k_inverse, k_gain, k_turned)
    q_low_grad = q_raw_grad.reshape(tok_rows, H * HD).astype(jnp.bfloat16)
    k_low_grad = k_raw_grad.reshape(tok_rows, KVH * HD).astype(jnp.bfloat16)
    v_low_grad = v_grad_tok.astype(jnp.bfloat16)
    q_wgrad = weight_grad(q_low_grad, normed_low)
    k_wgrad = weight_grad(k_low_grad, normed_low)
    v_wgrad = weight_grad(v_low_grad, normed_low)
    normed_one_grad = (
        spread_back(q_low_grad, q_full)
        + spread_back(k_low_grad, k_full)
        + spread_back(v_low_grad, v_full)
    )
    input_norm_grad, attn_gain_grad = rms_backward(
        hidden_in, inverse_one, attn_gain_f, normed_one_grad
    )
    input_grad = hidden_grad + input_norm_grad
    qk_grad = jnp.concatenate([q_gain_grad, k_gain_grad])
    q_out, k_out, v_out, o_out, attn_gain_out, ffn_gain_out, qk_out = (
        lax.psum_scatter(q_wgrad, ("blk", "uly"), scatter_dimension=0, tiled=True),
        lax.psum_scatter(k_wgrad, ("blk", "uly"), scatter_dimension=0, tiled=True),
        lax.psum_scatter(v_wgrad, ("blk", "uly"), scatter_dimension=0, tiled=True),
        lax.psum_scatter(out_wgrad, ("blk", "uly"), scatter_dimension=0, tiled=True),
        lax.psum_scatter(attn_gain_grad, ("blk", "uly"), scatter_dimension=0, tiled=True),
        lax.psum_scatter(ffn_gain_grad, ("blk", "uly"), scatter_dimension=0, tiled=True),
        lax.psum_scatter(qk_grad, ("blk", "uly"), scatter_dimension=0, tiled=True),
    )
    gate_out, up_out, down_out = (
        lax.psum_scatter(
            gate_wgrad.astype(jnp.bfloat16), "blk", scatter_dimension=0, tiled=True
        ).astype(jnp.float32),
        lax.psum_scatter(
            up_wgrad.astype(jnp.bfloat16), "blk", scatter_dimension=0, tiled=True
        ).astype(jnp.float32),
        lax.psum_scatter(
            down_wgrad.astype(jnp.bfloat16), "blk", scatter_dimension=0, tiled=True
        ).astype(jnp.float32),
    )
    return (
        output,
        input_grad,
        attn_gain_out,
        qk_out,
        q_out,
        k_out,
        v_out,
        o_out,
        ffn_gain_out,
        gate_out,
        up_out,
        down_out,
    )


def solution(mesh):
    return jax.shard_map(
        on_device,
        mesh=mesh,
        in_specs=(
            P(("blk", "uly"), None),
            P(),
            P(("blk", "uly")),
            P(("blk", "uly")),
            P(("blk", "uly"), None),
            P(("blk", "uly"), None),
            P(("blk", "uly"), None),
            P(("blk", "uly"), None),
            P(("blk", "uly")),
            P(("blk", "uly"), None),
            P(("blk", "uly"), None),
            P(("blk", "uly"), None),
            P(("blk", "uly"), None),
        ),
        out_specs=(
            P(("blk", "uly"), None),
            P(("blk", "uly"), None),
            P(("blk", "uly")),
            P(("blk", "uly")),
            P(("blk", "uly"), None),
            P(("blk", "uly"), None),
            P(("blk", "uly"), None),
            P(("blk", "uly"), None),
            P(("blk", "uly")),
            P(("blk", "uly"), None),
            P(("blk", "uly"), None),
            P(("blk", "uly"), None),
        ),
        check_vma=False,
    )
```

profile of v0, /device:TPU:0, one launch (start us, length us, event | category | flops | bytes accessed | tf_op | source)
XLA Modules:
  0.0 1949.3 jit_solution(15892296662127180622)
XLA Ops:
  13.1 42.2 %all-reduce.7 = (bf16[2048]{0:T(1024)(128)(2,1)S(1)}, bf16[128]{0:T(256)(128)(2,1)S(1)}, bf16[2048]{0:T(1024)(128)(2,1)S(1)}) all-reduce(bf16[2048]{0:T(1024)(128)(2,1)S(1)} %dynamic-update-slice, bf16[128]{0:T(256)(128)(2,1)S(1)} %dynamic-update-slice.1, ...), channel_id=1, replica_groups=mesh['blk'=8,'uly'=4] {'blk','uly'}, use_global_device_ids=true, to_apply=%add | all-reduce | flops 4224 | bytes 16896
  58.8 11.4 all-gather.10.cloned.1.call-done
  78.0 50.5 %all-gather.12.cloned.1.call-done = bf16[512,2048]{1,0:T(8,128)(2,1)} async-done(((bf16[16,2048]{1,0:T(8,128)(2,1)}), bf16[512,2048]{1,0:T(8,128)(2,1)}) %all-gather.12.cloned.1.call-update) | async-done | bytes 2097168 | tf_op jit(solution)/shard_map/all_gather | solution.py:103
  135.4 6.2 all-to-all-done.1
  143.6 4.0 collective-permute-start.1
  153.7 55.0 %all-gather.14.cloned.1.call-done = bf16[2048,2048]{1,0:T(8,128)(2,1)} async-done(((bf16[64,2048]{1,0:T(8,128)(2,1)}), bf16[2048,2048]{1,0:T(8,128)(2,1)}) %all-gather.14.cloned.1.call-update) | async-done | bytes 8388624 | tf_op jit(solution)/shard_map/all_gather | solution.py:101
  208.7 6.3 fusion.74
  218.1 3.6 all-to-all-start.2
  231.0 9.6 all-to-all-done.2
  241.3 19.8 %while.41 = (s32[]{:T(128)}, f32[512,2,4]{0,2,1:T(4,128)S(1)}, f32[512,2,4]{0,2,1:T(4,128)S(1)}, f32[512,2,4,64]{0,3,2,1:T(8,128)S(1)}, s32[5]{0:T(128)S(1)}, /*...) while((s32[]{:T(128)}, f32[512,2,4]{0,2,1:T(4,128)S(1)}, ...), condition=%wide.region_10.11_spmd.clone.clone, body=%wide.region_5.10_spmd.clone.clone.sunk | while | flops 561259520 | bytes 30425464 | solution.py:199
  243.8 7.6 conditional.8
  265.9 37.0 %all-gather.16.cloned.1.call-done = bf16[2048,2048]{1,0:T(8,128)(2,1)} async-done(((bf16[64,2048]{1,0:T(8,128)(2,1)}), bf16[2048,2048]{1,0:T(8,128)(2,1)}) %all-gather.16.cloned.1.call-update) | async-done | bytes 8388624 | tf_op jit(solution)/shard_map/all_gather | solution.py:104
  303.7 6.6 multiply_reduce_fusion.2
  313.8 43.4 %all-gather.20.cloned.1.call-done = bf16[2048,2048]{1,0:T(8,128)(2,1)} async-done(((bf16[256,2048]{1,0:T(8,128)(2,1)}), bf16[2048,2048]{1,0:T(8,128)(2,1)}) %all-gather.20.cloned.1.call-update) | async-done | bytes 8388624 | tf_op jit(solution)/shard_map/all_gather | solution.py:214
  357.2 48.0 %all-gather.18.cloned.1.call-done = bf16[512,2048]{1,0:T(8,128)(2,1)} async-done(((bf16[128,2048]{1,0:T(8,128)(2,1)}), bf16[512,2048]{1,0:T(8,128)(2,1)}) %all-gather.18.cloned.1.call-update) | async-done | bytes 2097168 | tf_op jit(solution)/shard_map/all_gather | solution.py:210
  405.1 10.5 fusion.83
  415.6 44.5 %all-gather.22.cloned.1.call-done = bf16[2048,2048]{1,0:T(8,128)(2,1)} async-done(((bf16[256,2048]{1,0:T(8,128)(2,1)}), bf16[2048,2048]{1,0:T(8,128)(2,1)}) %all-gather.22.cloned.1.call-update) | async-done | bytes 8388624 | tf_op jit(solution)/shard_map/all_gather | solution.py:215
  460.2 10.5 fusion.84
  470.6 37.1 %all-gather.26.cloned.1.call-done = bf16[512,2048]{1,0:T(8,128)(2,1)} async-done(((bf16[128,2048]{1,0:T(8,128)(2,1)}), bf16[512,2048]{1,0:T(8,128)(2,1)}) %all-gather.26.cloned.1.call-update) | async-done | bytes 2097168 | tf_op jit(solution)/shard_map/all_gather | solution.py:211
  507.7 55.0 %all-gather.24.cloned.1.call-done = bf16[2048,2048]{1,0:T(8,128)(2,1)} async-done(((bf16[256,2048]{1,0:T(8,128)(2,1)}), bf16[2048,2048]{1,0:T(8,128)(2,1)}) %all-gather.24.cloned.1.call-update) | async-done | bytes 8388624 | tf_op jit(solution)/shard_map/all_gather | solution.py:216
  562.7 14.0 multiply_convert_fusion
  576.7 8.5 fusion.85
  585.3 5.8 add_convert_fusion
  591.2 9.8 convolution_convert_fusion.3
  601.1 10.0 convolution_convert_fusion.2
  611.4 10.1 convolution_convert_fusion.1
  621.6 10.0 convolution_convert_fusion
  637.2 44.2 %reduce-scatter.10.cloned.1.call-done = bf16[128,2048]{1,0:T(8,128)(2,1)} async-done(((bf16[512,2048]{1,0:T(8,128)(2,1)}), bf16[128,2048]{1,0:T(8,128)(2,1)}) %reduce-scatter.10.cloned.1.call-update) | async-done | bytes 524304 | tf_op jit(solution)/shard_map/reduce_scatter | solution.py:224
  683.9 5.1 convolution_convert_fusion.4
  689.8 3.9 all-to-all-start.4
  693.8 14.6 all-to-all-done.4
  709.8 34.0 %while.42 = (s32[]{:T(128)}, f32[512,2,4,64]{0,3,2,1:T(8,128)S(1)}, f32[5,512,256]{2,1,0:T(8,128)}, s32[5]{0:T(128)S(1)}, s32[]{:T(128)}, /*index=5*/s32[512]{0:...) while((s32[]{:T(128)}, f32[512,2,4,64]{0,3,2,1:T(8,128)S(1)}, ...), condition=%wide.region_19.20_spmd.clone.clone, body=%wide.region_16.19_spmd.clone.clone.sunk | while | flops 1364657152 | bytes 75170736 | solution.py:298
  712.2 16.4 conditional.9
  713.2 4.5 fusion.82
  718.7 5.3 fusion.23
  751.3 13.4 collective-permute-done.4
  764.7 12.2 collective-permute-done.5
  785.0 4.8 all-to-all-done.6
  795.3 8.5 all_to_all.125
  806.8 8.1 fusion.62
  825.2 4.5 all-to-all-done.5
  842.7 11.0 fusion.72
  881.0 4.9 fusion.86
  888.2 81.9 %all-reduce.6 = (f32[2048]{0:T(1024)S(1)}, f32[128]{0:T(128)S(1)}, f32[2048]{0:T(1024)S(1)}) all-reduce(f32[2048]{0:T(1024)S(1)} %get-tuple-element.851, f32[128]{0:T(128)S(1)} %pad_maximum_fusion.5, f32[2048]{0:T(1024)S(1)} %copy-done.38), channel_id=4, replica_groups=mesh['blk'=8,'uly'=4] {'blk','uly'}, use_global_device_ids=true, to_apply=%region_24.25.clone | all-reduce | flops 4224 | bytes 33792
  981.7 79.7 %reduce-scatter.16.cloned.1.call-done = f32[16,2048]{1,0:T(8,128)} async-done(((f32[512,2048]{1,0:T(8,128)}), f32[16,2048]{1,0:T(8,128)}) %reduce-scatter.16.cloned.1.call-update) | async-done | bytes 131088 | tf_op jit(solution)/shard_map/reduce_scatter | solution.py:345
  1061.4 149.9 %reduce-scatter.18.cloned.1.call-done = f32[16,2048]{1,0:T(8,128)} async-done(((f32[512,2048]{1,0:T(8,128)}), f32[16,2048]{1,0:T(8,128)}) %reduce-scatter.18.cloned.1.call-update) | async-done | bytes 131088 | tf_op jit(solution)/shard_map/reduce_scatter | solution.py:346
  1211.3 366.0 %reduce-scatter.20.cloned.1.call-done = f32[64,2048]{1,0:T(8,128)} async-done(((f32[2048,2048]{1,0:T(8,128)}), f32[64,2048]{1,0:T(8,128)}) %reduce-scatter.20.cloned.1.call-update) | async-done | bytes 524304 | tf_op jit(solution)/shard_map/reduce_scatter | solution.py:347
  1577.3 365.0 %reduce-scatter.14.cloned.1.call-done = f32[64,2048]{1,0:T(8,128)} async-done(((f32[2048,2048]{1,0:T(8,128)}), f32[64,2048]{1,0:T(8,128)}) %reduce-scatter.14.cloned.1.call-update) | async-done | bytes 524304 | tf_op jit(solution)/shard_map/reduce_scatter | solution.py:344
  (362 shorter events, 181.9 us)
Async XLA Ops:
  7.2 121.4 %copy-start = (bf16[128,2048]{1,0:T(8,128)(2,1)S(1)}, bf16[128,2048]{1,0:T(8,128)(2,1)}, u32[]{:S(2)}) copy-start(bf16[128,2048]{1,0:T(8,128)(2,1)} %param.21) | copy-start | bytes 1572868
  7.2 63.1 %all-gather.10.cloned.1.call-start = ((), (), s32[]{:S(2)}) async-start(), calls=%async_computation.17 | async-start | bytes 2162688 | tf_op jit(solution)/shard_map/all_gather | solution.py:102
  7.9 120.6 %all-gather.12.cloned.1.call-start = ((), (), s32[]{:S(2)}) async-start(), calls=%async_computation.18 | async-start | bytes 2162688 | tf_op jit(solution)/shard_map/all_gather | solution.py:103
  8.7 200.0 %all-gather.14.cloned.1.call-start = ((), (), s32[]{:S(2)}) async-start(), calls=%async_computation.19 | async-start | bytes 8650752 | tf_op jit(solution)/shard_map/all_gather | solution.py:101
  9.4 293.5 %all-gather.16.cloned.1.call-start = ((), (), s32[]{:S(2)}) async-start(), calls=%async_computation.20 | async-start | bytes 8650752 | tf_op jit(solution)/shard_map/all_gather | solution.py:104
  10.0 347.2 %all-gather.20.cloned.1.call-start = ((), (), s32[]{:S(2)}) async-start(), calls=%async_computation.22 | async-start | bytes 9437184 | tf_op jit(solution)/shard_map/all_gather | solution.py:214
  55.4 153.3 %copy-start.29 = (f32[2048]{0:T(1024)}, f32[2048]{0:T(1024)S(1)}, u32[]{:S(2)}) copy-start(f32[2048]{0:T(1024)S(1)} %convert_element_type.191) | copy-start | bytes 24580
  58.0 150.7 %copy-start.39 = (f32[128]{0:T(128)}, f32[128]{0:T(128)S(1)}, u32[]{:S(2)}) copy-start(f32[128]{0:T(128)S(1)} %get-tuple-element.942) | copy-start | bytes 1540
  58.1 158.2 %copy-start.44 = (f32[64]{0:T(128)}, f32[64]{0:T(128)S(1)}, u32[]{:S(2)}) copy-start(f32[64]{0:T(128)S(1)} %get-tuple-element.945) | copy-start | bytes 772
  58.8 158.3 %copy-start.31 = (f32[128,32]{0,1:T(8,128)}, f32[128,32]{0,1:T(8,128)S(1)}, u32[]{:S(2)}) copy-start(f32[128,32]{0,1:T(8,128)S(1)} %get-tuple-element.940) | copy-start | bytes 49156
  70.3 64.9 %copy-start.46 = (s32[16]{0:T(128)S(1)}, s32[16]{0:T(128)}, u32[]{:S(2)}) copy-start(s32[16]{0:T(128)} %param.22) | copy-start | bytes 196
  72.9 142.1 %copy-start.15 = (f32[128,512]{1,0:T(8,128)}, f32[128,512]{1,0:T(8,128)S(1)}, u32[]{:S(2)}) copy-start(f32[128,512]{1,0:T(8,128)S(1)} %fusion.77) | copy-start | bytes 786436
  73.0 142.0 %copy-start.17 = (f32[128,512]{0,1:T(8,128)}, f32[128,512]{0,1:T(8,128)S(1)}, u32[]{:S(2)}) copy-start(f32[128,512]{0,1:T(8,128)S(1)} %copy.167) | copy-start | bytes 786436
  73.7 67.8 %copy-start.36 = (f32[128,8]{0,1:T(8,128)}, f32[128,8]{0,1:T(8,128)S(1)}, u32[]{:S(2)}) copy-start(f32[128,8]{0,1:T(8,128)S(1)} %get-tuple-element.937) | copy-start | bytes 12292
  74.5 57.1 %all-to-all-start = ((bf16[128,4,128]{0,2,1:T(8,128)(2,1)}), bf16[128,4,128]{0,2,1:T(8,128)(2,1)S(1)}, u32[]{:S(2)}, u32[]{:S(2)}) async-start(bf16[128,4,128]{0,2,1:T(8,128)(2,1)} %bitcast.29), calls=%async_computation | async-start | bytes 262144 | tf_op jit(solution)/shard_map/all_to_all | solution.py:136
  131.7 9.9 all-to-all-start.1
  141.6 80.2 %collective-permute-start = (bf16[512,256]{1,0:T(8,128)(2,1)S(1)}, bf16[512,256]{1,0:T(8,128)(2,1)}, u32[]{:S(2)}, u32[]{:S(2)}) collective-permute-start(bf16[512,256]{1,0:T(8,128)(2,1)S(1)} %pad_maximum_fusion.2), channel_id=1, source_target_pairs={{0,4},{4,8},{8,12},{12,16},{16,20},{20,24},{24,28},{1,5},{5,9},{9,... | collective-permute-start | bytes 786440 | tf_op jit(solution)/shard_map/ppermute | solution.py:20
  143.6 79.9 %collective-permute-start.1 = (bf16[512,256]{1,0:T(8,128)(2,1)S(1)}, bf16[512,256]{1,0:T(8,128)(2,1)}, u32[]{:S(2)}, u32[]{:S(2)}) collective-permute-start(bf16[512,256]{1,0:T(8,128)(2,1)S(1)} %pad_maximum_fusion.2), channel_id=1, source_target_pairs={{0,8},{4,12},{8,16},{12,20},{16,24},{20,28},{1,9},{5,13},{9,17},{1... | collective-permute-start | bytes 786440 | tf_op jit(solution)/shard_map/ppermute | solution.py:20
  147.6 77.6 %collective-permute-start.2 = (bf16[512,256]{1,0:T(8,128)(2,1)S(1)}, bf16[512,256]{1,0:T(8,128)(2,1)}, u32[]{:S(2)}, u32[]{:S(2)}) collective-permute-start(bf16[512,256]{1,0:T(8,128)(2,1)S(1)} %pad_maximum_fusion.2), channel_id=1, source_target_pairs={{0,12},{4,16},{8,20},{12,24},{16,28},{1,13},{5,17},{9,21},{13,25},... | collective-permute-start | bytes 786440 | tf_op jit(solution)/shard_map/ppermute | solution.py:20
  151.0 75.9 %collective-permute-start.3 = (bf16[512,256]{1,0:T(8,128)(2,1)S(1)}, bf16[512,256]{1,0:T(8,128)(2,1)}, u32[]{:S(2)}, u32[]{:S(2)}) collective-permute-start(bf16[512,256]{1,0:T(8,128)(2,1)S(1)} %pad_maximum_fusion.2), channel_id=1, source_target_pairs={{0,16},{4,20},{8,24},{12,28},{1,17},{5,21},{9,25},{13,29},{2,18},{... | collective-permute-start | bytes 786440 | tf_op jit(solution)/shard_map/ppermute | solution.py:20
  218.1 22.4 %all-to-all-start.2 = ((bf16[128,4,512]{0,2,1:T(8,128)(2,1)}), bf16[128,4,512]{0,2,1:T(8,128)(2,1)S(1)}, u32[]{:S(2)}, u32[]{:S(2)}) async-start(bf16[128,4,512]{0,2,1:T(8,128)(2,1)} %bitcast.260), calls=%async_computation.2 | async-start | bytes 1048576 | tf_op jit(solution)/shard_map/all_to_all | solution.py:135
  262.3 40.7 %all-to-all-start.3 = ((bf16[4,128,512]{1,2,0:T(8,128)(2,1)}), bf16[4,128,512]{1,2,0:T(8,128)(2,1)S(1)}, u32[]{:S(2)}, u32[]{:S(2)}) async-start(bf16[4,128,512]{1,2,0:T(8,128)(2,1)} %copy.173), calls=%async_computation.3 | async-start | bytes 1048576 | tf_op jit(solution)/shard_map/all_to_all | solution.py:205
  265.8 139.3 %all-gather.18.cloned.1.call-start = ((), (), s32[]{:S(2)}) async-start(), calls=%async_computation.21 | async-start | bytes 2621440 | tf_op jit(solution)/shard_map/all_gather | solution.py:210
  311.3 148.9 %all-gather.22.cloned.1.call-start = ((), (), s32[]{:S(2)}) async-start(), calls=%async_computation.23 | async-start | bytes 9437184 | tf_op jit(solution)/shard_map/all_gather | solution.py:215
  312.0 195.7 %all-gather.26.cloned.1.call-start = ((), (), s32[]{:S(2)}) async-start(), calls=%async_computation.26 | async-start | bytes 2621440 | tf_op jit(solution)/shard_map/all_gather | solution.py:211
  312.8 249.9 %all-gather.24.cloned.1.call-start = ((), (), s32[]{:S(2)}) async-start(), calls=%async_computation.24 | async-start | bytes 9437184 | tf_op jit(solution)/shard_map/all_gather | solution.py:216
  313.5 321.7 %reduce-scatter.12.cloned.1.call-start = ((), (), s32[]{:S(2)}) async-start(), calls=%async_computation.27 | async-start | bytes 2621440 | tf_op jit(solution)/shard_map/reduce_scatter | solution.py:241
  591.2 90.2 %reduce-scatter.10.cloned.1.call-start = ((), (), s32[]{:S(2)}) async-start(), calls=%async_computation.25 | async-start | bytes 2621440 | tf_op jit(solution)/shard_map/reduce_scatter | solution.py:224
  601.1 372.2 %reduce-scatter.22.cloned.1.call-start = ((), (), s32[]{:S(2)}) async-start(), calls=%async_computation.32 | async-start | bytes 9437184 | tf_op jit(solution)/shard_map/reduce_scatter | solution.py:353
  611.2 364.9 %reduce-scatter.24.cloned.1.call-start = ((), (), s32[]{:S(2)}) async-start(), calls=%async_computation.33 | async-start | bytes 9437184 | tf_op jit(solution)/shard_map/reduce_scatter | solution.py:356
  621.6 357.3 %reduce-scatter.26.cloned.1.call-start = ((), (), s32[]{:S(2)}) async-start(), calls=%async_computation.34 | async-start | bytes 9437184 | tf_op jit(solution)/shard_map/reduce_scatter | solution.py:359
  631.7 49.7 %copy-start.22 = (bf16[128,2048]{1,0:T(8,128)(2,1)S(1)}, bf16[128,2048]{1,0:T(8,128)(2,1)}, u32[]{:S(2)}) copy-start(bf16[128,2048]{1,0:T(8,128)(2,1)} %param.33) | copy-start | bytes 1572868
  689.8 18.5 all-to-all-start.4
  745.7 44.3 %copy-start.32 = (f32[128,32]{0,1:T(8,128)S(1)}, f32[128,32]{0,1:T(8,128)}, u32[]{:S(2)}) copy-start(f32[128,32]{0,1:T(8,128)} %copy-done.31) | copy-start | bytes 49156
  745.7 44.3 %copy-start.34 = (f32[128,32]{0,1:T(8,128)S(1)}, f32[128,32]{0,1:T(8,128)}, u32[]{:S(2)}) copy-start(f32[128,32]{0,1:T(8,128)} %get-tuple-element.938) | copy-start | bytes 49156
  745.7 44.3 %copy-start.18 = (f32[128,512]{0,1:T(8,128)S(1)}, f32[128,512]{0,1:T(8,128)}, u32[]{:S(2)}) copy-start(f32[128,512]{0,1:T(8,128)} %copy-done.17) | copy-start | bytes 786436
  745.7 45.5 %copy-start.16 = (f32[128,512]{1,0:T(8,128)S(1)}, f32[128,512]{1,0:T(8,128)}, u32[]{:S(2)}) copy-start(f32[128,512]{1,0:T(8,128)} %copy-done.15) | copy-start | bytes 786436
  745.8 18.9 collective-permute-start.4
  747.2 29.7 %collective-permute-start.5 = (bf16[512,256]{1,0:T(8,128)(2,1)S(1)}, bf16[512,256]{1,0:T(8,128)(2,1)S(1)}, u32[]{:S(2)}, u32[]{:S(2)}) collective-permute-start(bf16[512,256]{1,0:T(8,128)(2,1)S(1)} %get-tuple-element.917), channel_id=1, source_target_pairs={{8,0},{12,4},{16,8},{20,12},{24,16},{28,20},{9,1},{13,5},{17,9},{2... | collective-permute-start | bytes 786440 | tf_op jit(solution)/shard_map/ppermute | solution.py:20
  748.5 30.2 %collective-permute-start.6 = (bf16[512,256]{1,0:T(8,128)(2,1)S(1)}, bf16[512,256]{1,0:T(8,128)(2,1)S(1)}, u32[]{:S(2)}, u32[]{:S(2)}) collective-permute-start(bf16[512,256]{1,0:T(8,128)(2,1)S(1)} %get-tuple-element.916), channel_id=1, source_target_pairs={{12,0},{16,4},{20,8},{24,12},{28,16},{13,1},{17,5},{21,9},{25,13},... | collective-permute-start | bytes 786440 | tf_op jit(solution)/shard_map/ppermute | solution.py:20
  749.9 28.9 %collective-permute-start.7 = (bf16[512,256]{1,0:T(8,128)(2,1)S(1)}, bf16[512,256]{1,0:T(8,128)(2,1)S(1)}, u32[]{:S(2)}, u32[]{:S(2)}) collective-permute-start(bf16[512,256]{1,0:T(8,128)(2,1)S(1)} %get-tuple-element.915), channel_id=1, source_target_pairs={{16,0},{20,4},{24,8},{28,12},{17,1},{21,5},{25,9},{29,13},{18,2},{... | collective-permute-start | bytes 786440 | tf_op jit(solution)/shard_map/ppermute | solution.py:20
  780.6 9.2 all-to-all-start.6
  783.9 277.5 %reduce-scatter.16.cloned.1.call-start = ((), (), s32[]{:S(2)}) async-start(), calls=%async_computation.29 | async-start | bytes 4325376 | tf_op jit(solution)/shard_map/reduce_scatter | solution.py:345
  795.2 416.1 %reduce-scatter.18.cloned.1.call-start = ((), (), s32[]{:S(2)}) async-start(), calls=%async_computation.30 | async-start | bytes 4325376 | tf_op jit(solution)/shard_map/reduce_scatter | solution.py:346
  806.7 770.6 %reduce-scatter.20.cloned.1.call-start = ((), (), s32[]{:S(2)}) async-start(), calls=%async_computation.31 | async-start | bytes 17301504 | tf_op jit(solution)/shard_map/reduce_scatter | solution.py:347
  816.0 13.7 all-to-all-start.5
  819.5 1122.8 %reduce-scatter.14.cloned.1.call-start = ((), (), s32[]{:S(2)}) async-start(), calls=%async_computation.28 | async-start | bytes 17301504 | tf_op jit(solution)/shard_map/reduce_scatter | solution.py:344
  885.9 85.9 %copy-start.45 = (f32[128]{0:T(128)S(1)}, f32[128]{0:T(128)}, u32[]{:S(2)}) copy-start(f32[128]{0:T(128)} %get-tuple-element.941) | copy-start | bytes 1540
  (37 other events, 430.3 us)
Sparse Core Ops, SparseCore 0:
  11.0 59.2 all-gather.9
  73.2 55.3 all-gather.11
  131.5 77.1 all-gather.13
  211.5 91.3 all-gather.15
  304.7 52.4 all-gather.19
  359.2 45.9 all-gather.17
  407.0 53.0 all-gather.21
  461.7 45.9 all-gather.25
  509.6 53.0 all-gather.23
  591.3 43.8 reduce-scatter.11
  638.2 43.1 reduce-scatter.9
  684.6 70.5 reduce-scatter.21
  759.1 76.7 reduce-scatter.23
  839.3 71.2 reduce-scatter.25
  913.4 147.9 reduce-scatter.15
  1064.2 147.0 reduce-scatter.17
  1214.1 363.1 reduce-scatter.19
  1580.1 362.1 reduce-scatter.13
where the time goes:
time: 1960 us; the launch traced here: 1950 us
  waiting for transfers between devices  1460 us (74%)
  matrix products  161 us (8%)
  blocking collectives  133 us (7%)
  local copies, waits for them, and re-layouts  79.9 us (4%)
  starting transfers between devices  42.9 us (2%)
  other arithmetic  39.4 us (2%)
    reduce_scatter x1, waiting for transfers between devices, on_device(): lax.psum_scatter(out_wgrad, ('blk', 'uly'), scatter_dimension=0, tiled=True)  366 us
    reduce_scatter x1, waiting for transfers between devices, on_device(): lax.psum_scatter(q_wgrad, ('blk', 'uly'), scatter_dimension=0, tiled=True)  365 us
    reduce_scatter x1, waiting for transfers between devices, on_device(): lax.psum_scatter(v_wgrad, ('blk', 'uly'), scatter_dimension=0, tiled=True)  150 us
    unnamed x2, blocking collectives  124 us
    reduce_scatter x1, waiting for transfers between devices, on_device(): lax.psum_scatter(k_wgrad, ('blk', 'uly'), scatter_dimension=0, tiled=True)  79.7 us
    all_gather x1, waiting for transfers between devices, on_device(): lax.all_gather(down_weight, 'blk', axis=0, tiled=True)  55 us
    all_gather x1, waiting for transfers between devices, on_device(): lax.all_gather(q_weight, ('blk', 'uly'), axis=0, tiled=True)  55 us
    dot_general x7, matrix products, weight_grad(): lax.dot_general(upstream, inputs, (((0,), (0,)), ((), ())), preferred_ele...  54.9 us
  transfers between devices with their start and end apart: 33, of which 23 were waited for; matrix products, arithmetic and copies ran while one was open for 13% of the time, Pallas kernels for 0%

commit v1 on v0

v1 whole, which is shorter than its diff:
```python
import functools

import jax
import jax.numpy as jnp
from jax import lax
from jax.experimental import pallas as pl
from jax.experimental.pallas import tpu as pltpu
from jax.sharding import Mesh
from jax.sharding import PartitionSpec as P

H = 32
KVH = 8
HD = 64
GROUP = H // KVH
PAIR = 2 * HD
QB = 128
KB = 256

NORM_EPSILON = 1e-05
ROPE_THETA = 1000000.0
SCALE = HD**-0.5

ALL = ("y", "x", "c", "r", "z")
HEADS = ("y", "x", "c")
SPREAD = ("r", "z")
TOKS = ("y", "z")
HIDDEN = ("x", "c", "r")

F32 = jnp.float32
BF16 = jnp.bfloat16
VMEM_LIMIT = 60 << 20


def dot_nt(a, b):
    return lax.dot_general(a, b, (((1,), (1,)), ((), ())), preferred_element_type=F32)


def dot_nn(a, b):
    return lax.dot_general(a, b, (((1,), (0,)), ((), ())), preferred_element_type=F32)


def dot_tn(a, b):
    return lax.dot_general(a, b, (((0,), (0,)), ((), ())), preferred_element_type=F32)


def rms_forward(values, gain):
    inverse = lax.rsqrt(jnp.mean(values * values, axis=-1, keepdims=True) + NORM_EPSILON)
    return (values * inverse * gain, inverse)


def rms_backward(values, inverse, gain, upstream):
    scaled = upstream * gain
    gain_grad = jnp.sum((upstream * values * inverse).reshape(-1, values.shape[-1]), axis=0)
    values_grad = inverse * scaled - values * inverse**3 * jnp.mean(
        scaled * values, axis=-1, keepdims=True
    )
    return (values_grad, gain_grad)


def rotate(values, cosine, sine):
    half_width = values.shape[-1] // 2
    front_half = values[..., :half_width]
    back_half = values[..., half_width:]
    return jnp.concatenate(
        [front_half * cosine - back_half * sine, back_half * cosine + front_half * sine], axis=-1
    )


def doc_start_of(row_ids, doc_starts):
    return jnp.max(
        jnp.where(doc_starts[None, :] <= row_ids[:, None], doc_starts[None, :], 0), axis=1
    )


def first_key_block(doc_ref, ndoc, row):
    start = jnp.int32(0)
    for i in range(ndoc):
        d = doc_ref[i]
        start = jnp.where(d <= row, d, start)
    return start


def doc_start_rows(doc_ref, ndoc, rows):
    start = jnp.zeros(rows.shape, jnp.int32)
    for i in range(ndoc):
        d = doc_ref[i]
        start = jnp.where(d <= rows, d, start)
    return start


def prepare_keys(kv_ref, k0, k1, v0, v1, fill):
    kv = kv_ref[...]
    turned = jnp.concatenate([kv[:, HD:], kv[:, :HD]], axis=1)
    low_half = lax.broadcasted_iota(jnp.int32, kv.shape, 1) < HD
    zero = jnp.zeros_like(kv)
    other = jnp.full_like(kv, fill)
    k0[...] = jnp.where(low_half, kv, zero)
    k1[...] = jnp.where(low_half, zero, turned)
    v0[...] = jnp.where(low_half, turned, other)
    v1[...] = jnp.where(low_half, other, kv)


def attend_kernel(ndoc, stride, doc_ref, at_ref, q_ref, kv_ref, o_ref, of_ref, l_ref, k0, k1, v0, v1, even, odd):
    step = pl.program_id(0)

    @pl.when(step == 0)
    def _():
        prepare_keys(kv_ref, k0, k1, v0, v1, 1.0)

    base = (step * stride + at_ref[0]) * QB
    first = first_key_block(doc_ref, ndoc, base) // KB
    last_doc = first_key_block(doc_ref, ndoc, base + QB - 1)
    last = (base + QB - 1) // KB
    queries = jnp.concatenate([q_ref[:, :PAIR], q_ref[:, PAIR:]], axis=0)
    rows = base + lax.broadcasted_iota(jnp.int32, (QB, 1), 0)
    start = doc_start_rows(doc_ref, ndoc, rows)
    rows = jnp.concatenate([rows, rows], axis=0)
    start = jnp.concatenate([start, start], axis=0)
    even[...] = jnp.zeros_like(even)
    odd[...] = jnp.zeros_like(odd)

    def block(j, masked):
        at = pl.ds(pl.multiple_of(j * KB, KB), KB)
        for keys, values, acc in ((k0, v0, even), (k1, v1, odd)):
            p = jnp.exp(dot_nt(queries, keys[at, :]))
            if masked:
                cols = j * KB + lax.broadcasted_iota(jnp.int32, p.shape, 1)
                p = jnp.where((cols >= start) & (cols <= rows), p, 0.0)
            acc[...] += dot_nn(p.astype(BF16), values[at, :])

    def body(j, carry):
        whole = (j * KB >= last_doc) & (j * KB + KB - 1 <= base)

        @pl.when(whole)
        def _():
            block(j, False)

        @pl.when(jnp.logical_not(whole))
        def _():
            block(j, True)

        return carry

    lax.fori_loop(first, last + 1, body, 0)
    low_half = lax.broadcasted_iota(jnp.int32, even.shape, 1) < HD
    ev, od = even[...], odd[...]
    total = jnp.where(low_half, od, ev)
    total = jnp.concatenate([total[:, HD:], total[:, :HD]], axis=1)
    mixed = jnp.where(low_half, ev, od) / total
    minus_log = -jnp.log(total)
    for pair in range(2):
        part = mixed[pair * QB : (pair + 1) * QB]
        o_ref[:, pair * PAIR : (pair + 1) * PAIR] = part.astype(BF16)
        of_ref[:, pair * PAIR : (pair + 1) * PAIR] = part
        turned = jnp.transpose(minus_log[pair * QB : (pair + 1) * QB])
        l_ref[0, pair : pair + 1, :] = turned[0:1]
        l_ref[0, pair + 2 : pair + 3, :] = turned[HD : HD + 1]


def attend(doc_starts, at, q, kv, stride):
    rows, width = q.shape
    steps = rows // QB
    keys = kv.shape[0]
    ndoc = doc_starts.shape[0]
    row_block = lambda i, *_: (i, 0)
    return pl.pallas_call(
        functools.partial(attend_kernel, ndoc, stride),
        out_shape=(
            jax.ShapeDtypeStruct((rows, width), BF16),
            jax.ShapeDtypeStruct((rows, width), F32),
            jax.ShapeDtypeStruct((steps, GROUP, QB), F32),
        ),
        grid_spec=pltpu.PrefetchScalarGridSpec(
            num_scalar_prefetch=2,
            grid=(steps,),
            in_specs=[
                pl.BlockSpec((QB, width), row_block),
                pl.BlockSpec((keys, PAIR), lambda i, *_: (0, 0), pipeline_mode=pl.Buffered(1)),
            ],
            out_specs=[
                pl.BlockSpec((QB, width), row_block),
                pl.BlockSpec((QB, width), row_block),
                pl.BlockSpec((1, GROUP, QB), lambda i, *_: (i, 0, 0)),
            ],
            scratch_shapes=[pltpu.VMEM((keys, PAIR), BF16)] * 4 + [pltpu.VMEM((2 * QB, PAIR), F32)] * 2,
        ),
        compiler_params=pltpu.CompilerParams(vmem_limit_bytes=VMEM_LIMIT),
        cost_estimate=pl.CostEstimate(flops=2 * rows * 1024 * width * 2, bytes_accessed=8 << 20, transcendentals=rows * 4096),
        name="attend",
    )(doc_starts, at, q, kv)


def attend_back_kernel(
    ndoc, stride, doc_ref, at_ref, q_ref, do_ref, of_ref, l_ref, kv_ref, dq_ref, dkv_ref, k0, k1, v0, v1, dk, dv, dq
):
    step = pl.program_id(0)

    @pl.when(step == 0)
    def _():
        prepare_keys(kv_ref, k0, k1, v0, v1, 0.0)
        dk[...] = jnp.zeros_like(dk)
        dv[...] = jnp.zeros_like(dv)

    base = (step * stride + at_ref[0]) * QB
    first = first_key_block(doc_ref, ndoc, base) // KB
    last_doc = first_key_block(doc_ref, ndoc, base + QB - 1)
    last = (base + QB - 1) // KB
    queries = jnp.concatenate([q_ref[:, :PAIR], q_ref[:, PAIR:]], axis=0)
    grads = jnp.concatenate([do_ref[:, :PAIR], do_ref[:, PAIR:]], axis=0)
    low_half = lax.broadcasted_iota(jnp.int32, queries.shape, 1) < HD
    zero = jnp.zeros_like(queries)
    both_q = jnp.concatenate([jnp.where(low_half, queries, zero), jnp.where(low_half, zero, queries)], axis=0)
    both_g = jnp.concatenate([jnp.where(low_half, grads, zero), jnp.where(low_half, zero, grads)], axis=0)
    minus_log, delta = [], []
    for pair in range(2):
        at = slice(pair * PAIR, (pair + 1) * PAIR)
        product = jnp.transpose(do_ref[:, at].astype(F32) * of_ref[:, at])
        delta.append(
            (jnp.sum(product[:HD], axis=0, keepdims=True), jnp.sum(product[HD:], axis=0, keepdims=True))
        )
    minus_log = [
        jnp.concatenate([l_ref[0, 0:1, :], l_ref[0, 1:2, :]], axis=1),
        jnp.concatenate([l_ref[0, 2:3, :], l_ref[0, 3:4, :]], axis=1),
    ]
    delta = [jnp.concatenate([delta[0][half], delta[1][half]], axis=1) for half in range(2)]
    rows = base + lax.broadcasted_iota(jnp.int32, (1, QB), 1)
    start = doc_start_rows(doc_ref, ndoc, rows)
    rows = jnp.concatenate([rows, rows], axis=1)
    start = jnp.concatenate([start, start], axis=1)
    dq[...] = jnp.zeros_like(dq)

    def block(j, masked):
        at = pl.ds(pl.multiple_of(j * KB, KB), KB)
        probs, scores = [], []
        for half, keys, values in ((0, k0, v0), (1, k1, v1)):
            p = jnp.exp(dot_nt(keys[at, :], queries) + minus_log[half])
            if masked:
                cols = j * KB + lax.broadcasted_iota(jnp.int32, p.shape, 0)
                p = jnp.where((cols >= start) & (cols <= rows), p, 0.0)
            ds = (p * (dot_nt(values[at, :], grads) - delta[half])).astype(BF16)
            probs.append(p.astype(BF16))
            scores.append(ds)
        dv[at, :] += dot_nn(jnp.concatenate(probs, axis=1), both_g)
        dk[at, :] += dot_nn(jnp.concatenate(scores, axis=1), both_q)
        dq[...] += dot_tn(scores[0], k0[at, :]) + dot_tn(scores[1], k1[at, :])

    def body(j, carry):
        whole = (j * KB >= last_doc) & (j * KB + KB - 1 <= base)

        @pl.when(whole)
        def _():
            block(j, False)

        @pl.when(jnp.logical_not(whole))
        def _():
            block(j, True)

        return carry

    lax.fori_loop(first, last + 1, body, 0)
    dq_ref[:, :PAIR] = dq[:QB] * SCALE
    dq_ref[:, PAIR:] = dq[QB:] * SCALE

    @pl.when(step == pl.num_programs(0) - 1)
    def _():
        gk, gv = dk[...], dv[...]
        gk = gk + jnp.concatenate([gk[:, HD:], gk[:, :HD]], axis=1)
        gv = gv + jnp.concatenate([gv[:, HD:], gv[:, :HD]], axis=1)
        half = lax.broadcasted_iota(jnp.int32, gk.shape, 1) < HD
        dkv_ref[...] = jnp.where(half, gk, gv).astype(BF16)


def attend_back(doc_starts, at, q, do, of, logs, kv, stride):
    rows, width = q.shape
    steps = rows // QB
    keys = kv.shape[0]
    ndoc = doc_starts.shape[0]
    row_block = lambda i, *_: (i, 0)
    return pl.pallas_call(
        functools.partial(attend_back_kernel, ndoc, stride),
        out_shape=(
            jax.ShapeDtypeStruct((rows, width), F32),
            jax.ShapeDtypeStruct((keys, PAIR), BF16),
        ),
        grid_spec=pltpu.PrefetchScalarGridSpec(
            num_scalar_prefetch=2,
            grid=(steps,),
            in_specs=[
                pl.BlockSpec((QB, width), row_block),
                pl.BlockSpec((QB, width), row_block),
                pl.BlockSpec((QB, width), row_block),
                pl.BlockSpec((1, GROUP, QB), lambda i, *_: (i, 0, 0)),
                pl.BlockSpec((keys, PAIR), lambda i, *_: (0, 0), pipeline_mode=pl.Buffered(1)),
            ],
            out_specs=[
                pl.BlockSpec((QB, width), row_block),
                pl.BlockSpec((keys, PAIR), lambda i, *_: (0, 0), pipeline_mode=pl.Buffered(1)),
            ],
            scratch_shapes=[pltpu.VMEM((keys, PAIR), BF16)] * 4
            + [pltpu.VMEM((keys, PAIR), F32)] * 2
            + [pltpu.VMEM((2 * QB, PAIR), F32)],
        ),
        compiler_params=pltpu.CompilerParams(vmem_limit_bytes=VMEM_LIMIT),
        cost_estimate=pl.CostEstimate(flops=2 * rows * 1024 * width * 5, bytes_accessed=12 << 20, transcendentals=rows * 4096),
        name="attend_back",
    )(doc_starts, at, q, do, of, logs, kv)


def gather(value, axes, axis=0):
    return lax.all_gather(value, axes, axis=axis, tiled=True)


def scatter_sum(value, axes, axis=0):
    return lax.psum_scatter(value, axes, scatter_dimension=axis, tiled=True)


def on_device(
    tokens,
    doc_starts,
    attn_gain,
    qk_gains,
    q_weight,
    k_weight,
    v_weight,
    out_weight,
    ffn_gain,
    gate_weight,
    up_weight,
    down_weight,
    out_grad,
):
    spread = lax.axis_size("r") * lax.axis_size("z")
    place = lax.axis_index("r") * lax.axis_size("z") + lax.axis_index("z")
    at = jnp.reshape(place, (1,)).astype(jnp.int32)
    toks, width = tokens.shape
    heads = KVH
    rows = heads * toks
    q_rows, k_rows = q_weight.shape[0], k_weight.shape[0]

    own_gains = jnp.concatenate([attn_gain, ffn_gain, qk_gains])
    gains = gather(own_gains[None], ALL).astype(F32)
    n_gain, n_qk = attn_gain.shape[0], qk_gains.shape[0]
    attn_gain_f = gains[:, :n_gain].reshape(-1)
    ffn_gain_f = gains[:, n_gain : 2 * n_gain].reshape(-1)
    qk_gain_f = gains[:, 2 * n_gain :].reshape(-1)
    q_gain, k_gain = qk_gain_f[:HD], qk_gain_f[HD:]

    all_tokens = gather(tokens, HEADS)
    qkv_weight = gather(jnp.concatenate([q_weight, k_weight, v_weight], axis=0)[None], SPREAD)
    qkv_weight = jnp.concatenate(
        [
            qkv_weight[:, :q_rows].reshape(-1, width),
            qkv_weight[:, q_rows : q_rows + k_rows].reshape(-1, width),
            qkv_weight[:, q_rows + k_rows :].reshape(-1, width),
        ],
        axis=0,
    )
    o_weight = gather(out_weight, SPREAD)
    normed, _ = rms_forward(all_tokens.astype(F32), attn_gain_f)
    normed = normed.astype(BF16)
    qkv = dot_nt(normed, qkv_weight)
    q_width = GROUP * HD
    row_ids = (
        (jnp.arange(heads, dtype=jnp.int32)[:, None] * spread + place) * toks
        + jnp.arange(toks, dtype=jnp.int32)[None, :]
    ).reshape(-1)
    positions = (row_ids - doc_start_of(row_ids, doc_starts)).astype(F32)
    frequency = ROPE_THETA ** (-jnp.arange(HD // 2, dtype=F32) * 2.0 / HD)
    angle = positions[:, None] * frequency[None, :]
    cosine = jnp.cos(angle)[:, None, :]
    sine = jnp.sin(angle)[:, None, :]
    q_heads = qkv[:, :q_width].reshape(rows, GROUP, HD)
    k_heads = qkv[:, q_width : q_width + HD].reshape(rows, 1, HD)
    q_normed, q_inverse = rms_forward(q_heads, q_gain)
    k_normed, k_inverse = rms_forward(k_heads, k_gain)
    queries = rotate(q_normed, cosine, sine).reshape(rows, q_width).astype(BF16) * BF16(SCALE)
    keys = rotate(k_normed, cosine, sine).reshape(rows, HD).astype(BF16)
    own_kv = jnp.concatenate([keys, qkv[:, q_width + HD :].astype(BF16)], axis=1)
    kv = gather(own_kv[None], SPREAD).reshape(spread, heads, toks, PAIR)
    kv = jnp.swapaxes(kv, 0, 1).reshape(spread * rows, PAIR)
    mixed, mixed_f, logs = attend(doc_starts, at, queries, kv, spread)

    all_mixed = gather(mixed, HEADS, axis=1)
    projected = dot_nt(all_mixed, o_weight).astype(BF16)
    projected = lax.all_to_all(projected, HEADS, split_axis=0, concat_axis=1, tiled=True)
    hidden_in = tokens.astype(F32)
    hidden = hidden_in + projected.astype(F32)
    normed_two, inverse_two = rms_forward(hidden, ffn_gain_f)

    gate_rows = gather(gate_weight, HIDDEN)
    up_rows = gather(up_weight, HIDDEN)
    down_rows = gather(down_weight, HIDDEN)
    ffn_in = gather(normed_two.astype(BF16), TOKS)
    ffn_grad = gather(out_grad, TOKS)
    gate = dot_nt(ffn_in, gate_rows)
    upward = dot_nt(ffn_in, up_rows)
    sigmoid_gate = jax.nn.sigmoid(gate)
    silu_gate = gate * sigmoid_gate
    active = (silu_gate * upward).astype(BF16)
    active_grad = dot_nt(ffn_grad, down_rows)
    silu_slope = sigmoid_gate * (1.0 + gate * (1.0 - sigmoid_gate))
    gate_grad = (active_grad * upward * silu_slope).astype(BF16)
    up_grad = (active_grad * silu_gate).astype(BF16)
    ffn_in_grad = (dot_nn(gate_grad, gate_rows) + dot_nn(up_grad, up_rows)).astype(BF16)
    ffn_in_grad = scatter_sum(ffn_in_grad, TOKS).astype(F32)
    ffn_out = scatter_sum(dot_nn(active, down_rows).astype(BF16), TOKS).astype(F32)
    output = hidden + ffn_out
    gate_out = scatter_sum(dot_tn(gate_grad, ffn_in).astype(BF16), HIDDEN).astype(F32)
    up_out = scatter_sum(dot_tn(up_grad, ffn_in).astype(BF16), HIDDEN).astype(F32)
    down_out = scatter_sum(dot_tn(active, ffn_grad).astype(BF16), HIDDEN).astype(F32)

    norm_grad, ffn_gain_grad = rms_backward(hidden, inverse_two, ffn_gain_f, ffn_in_grad)
    hidden_grad = out_grad.astype(F32) + norm_grad
    hidden_low = hidden_grad.astype(BF16)
    grad_cols = lax.all_to_all(hidden_low, HEADS, split_axis=1, concat_axis=0, tiled=True)
    mixed_grad = scatter_sum(dot_nn(grad_cols, o_weight).astype(BF16), HEADS, axis=1)
    out_wgrad = dot_tn(grad_cols, all_mixed)
    o_out = scatter_sum(out_wgrad.astype(BF16), SPREAD).astype(F32)
    q_grad, kv_grad = attend_back(doc_starts, at, queries, mixed_grad, mixed_f, logs, kv, spread)
    kv_grad = jnp.swapaxes(kv_grad.reshape(heads, spread, toks, PAIR), 0, 1)
    kv_grad = scatter_sum(kv_grad.reshape(spread * rows, PAIR), SPREAD)

    q_turned = rotate(q_grad.reshape(rows, GROUP, HD), cosine, -sine)
    k_turned = rotate(kv_grad[:, :HD].astype(F32).reshape(rows, 1, HD), cosine, -sine)
    q_raw_grad, q_gain_grad = rms_backward(q_heads, q_inverse, q_gain, q_turned)
    k_raw_grad, k_gain_grad = rms_backward(k_heads, k_inverse, k_gain, k_turned)
    qkv_grad = jnp.concatenate(
        [q_raw_grad.reshape(rows, q_width), k_raw_grad.reshape(rows, HD)], axis=1
    ).astype(BF16)
    qkv_grad = jnp.concatenate([qkv_grad, kv_grad[:, HD:]], axis=1)
    normed_grad = scatter_sum(dot_nn(qkv_grad, qkv_weight).astype(BF16), HEADS).astype(F32)
    qkv_wgrad = dot_tn(qkv_grad, normed).astype(BF16)
    qkv_wgrad = jnp.concatenate(
        [
            qkv_wgrad[:q_width].reshape(spread, q_rows, width),
            qkv_wgrad[q_width : q_width + HD].reshape(spread, k_rows, width),
            qkv_wgrad[q_width + HD :].reshape(spread, k_rows, width),
        ],
        axis=1,
    )
    qkv_out = scatter_sum(qkv_wgrad, SPREAD)[0].astype(F32)
    _, inverse_one = rms_forward(hidden_in, attn_gain_f)
    input_norm_grad, attn_gain_grad = rms_backward(hidden_in, inverse_one, attn_gain_f, normed_grad)
    input_grad = hidden_grad + input_norm_grad
    members = attn_gain_grad.shape[0] // n_gain
    gain_grads = jnp.concatenate(
        [
            attn_gain_grad.reshape(members, n_gain),
            ffn_gain_grad.reshape(members, n_gain),
            jnp.concatenate([q_gain_grad, k_gain_grad]).reshape(members, n_qk),
        ],
        axis=1,
    )
    gain_out = scatter_sum(gain_grads, ALL)[0]
    return (
        output,
        input_grad,
        gain_out[:n_gain],
        gain_out[2 * n_gain :],
        qkv_out[:q_rows],
        qkv_out[q_rows : q_rows + k_rows],
        qkv_out[q_rows + k_rows :],
        o_out,
        gain_out[n_gain : 2 * n_gain],
        gate_out,
        up_out,
        down_out,
    )


def solution(mesh):
    blocks, spread = mesh.shape["blk"], mesh.shape["uly"]
    fine = Mesh(mesh.devices.reshape(2, 2, 2, blocks // 8, spread), ALL)
    by_rows, by_one = P(ALL, None), P(ALL)
    return jax.shard_map(
        on_device,
        mesh=fine,
        in_specs=(
            by_rows,
            P(),
            by_one,
            by_one,
            by_rows,
            by_rows,
            by_rows,
            by_rows,
            by_one,
            by_rows,
            by_rows,
            by_rows,
            by_rows,
        ),
        out_specs=(
            by_rows,
            by_rows,
            by_one,
            by_one,
            by_rows,
            by_rows,
            by_rows,
            by_rows,
            by_one,
            by_rows,
            by_rows,
            by_rows,
        ),
        check_vma=False,
    )
```

time: 1960 us -> 1070 us (0.55)
  waiting for transfers between devices: 1460 us -> 709 us
  matrix products: 161 us -> 108 us
  local copies, waits for them, and re-layouts: 79.9 us -> 32.8 us
  Pallas kernels: 0 us -> 46.7 us
  starting transfers between devices: 42.9 us -> 5.29 us
  blocking collectives: 133 us -> 99.7 us
    reduce_scatter x9 -> x10, waiting for transfers between devices: 1010 us -> 378 us  [scatter_sum(): return lax.psum_scatter(value, axes, scatter_dimension=axis, tiled=True)]
    all_gather x9 -> x10, waiting for transfers between devices: 382 us -> 312 us  [gather(): return lax.all_gather(value, axes, axis=axis, tiled=True)]
    dot_general x28 -> x15, matrix products: 161 us -> 108 us  [the longest x5 39.8 us: dot_nt(): lax.dot_general(a, b, (((1,), (1,)), ((), ())), preferred_element_type=F32)]
    pallas_call x0 -> x2, Pallas kernels: none -> 46.7 us  [the longest x1 24.4 us: attend_back(): pl.pallas_call(functools.partial(attend_back_kernel, ndoc, stride), out_s...]
    unnamed x2, blocking collectives: 124 us -> 86.5 us
    ppermute x8 -> x0, waiting for transfers between devices: 27.4 us -> none  [shifted(): return lax.ppermute(value, axis, pairs)]
    all_to_all x7 -> x1, waiting for transfers between devices: 39.6 us -> 15.2 us  [on_device(): lax.all_to_all(projected, HEADS, split_axis=0, concat_axis=1, tiled=True)]
    all_to_all x7 -> x1, starting transfers between devices: 24.8 us -> 3.63 us  [on_device(): lax.all_to_all(projected, HEADS, split_axis=0, concat_axis=1, tiled=True)]
  transfers between devices with their start and end apart: 33 -> 21, of which waited for: 23 -> 19; matrix products, arithmetic and copies ran while one was open for 13% -> 12% of each run, Pallas kernels for 0% -> 2%
where the time goes in v1:
time: 1070 us; the launch traced here: 1060 us
  waiting for transfers between devices  709 us (66%)
  matrix products  108 us (10%)
  blocking collectives  99.7 us (9%)
  Pallas kernels  46.7 us (4%)
  other arithmetic  38.1 us (4%)
  local copies, waits for them, and re-layouts  32.8 us (3%)
  between operations  15.3 us (1%)
    reduce_scatter x10, waiting for transfers between devices, scatter_sum(): return lax.psum_scatter(value, axes, scatter_dimension=axis, tiled=True)  378 us
    all_gather x10, waiting for transfers between devices, gather(): return lax.all_gather(value, axes, axis=axis, tiled=True)  312 us
    unnamed x2, blocking collectives  86.5 us
    dot_general x5, matrix products, dot_nt(): lax.dot_general(a, b, (((1,), (1,)), ((), ())), preferred_element_type=F32)  39.8 us
    dot_general x5, matrix products, dot_tn(): lax.dot_general(a, b, (((0,), (0,)), ((), ())), preferred_element_type=F32)  37.2 us
    dot_general x5, matrix products, dot_nn(): lax.dot_general(a, b, (((1,), (0,)), ((), ())), preferred_element_type=F32)  31.3 us
    pallas_call x1, Pallas kernels, attend_back(): pl.pallas_call(functools.partial(attend_back_kernel, ndoc, stride), out_s...  24.4 us
    pallas_call x1, Pallas kernels, attend(): pl.pallas_call(functools.partial(attend_kernel, ndoc, stride), out_shape=...  22.2 us
  transfers between devices with their start and end apart: 21, of which 19 were waited for; matrix products, arithmetic and copies ran while one was open for 12% of the time, Pallas kernels for 2%

profile of v1, /device:TPU:0, one launch (start us, length us, event | category | flops | bytes accessed | tf_op | source)
XLA Modules:
  0.0 1055.5 jit_solution(2980096904580225863)
XLA Ops:
  10.8 44.5 %all-reduce = bf16[4224]{0:T(1024)(128)(2,1)S(1)} all-reduce(bf16[4224]{0:T(1024)(128)(2,1)S(1)} %dynamic-update-slice), channel_id=2, replica_groups=mesh['y'=2,'x'=2,'c'=2,'r'=1,'z'=4] {'y','x','c','r','z'}, use_global_device_ids=true, to_apply=%add | all-reduce | flops 4224 | bytes 16896
  59.4 29.1 %all-gather.14.cloned.1.call-done = bf16[1024,2048]{1,0:T(8,128)(2,1)} async-done(((bf16[128,2048]{1,0:T(8,128)(2,1)}), bf16[1024,2048]{1,0:T(8,128)(2,1)}) %all-gather.14.cloned.1.call-update) | async-done | bytes 4194320 | tf_op jit(solution)/shard_map/all_gather | solution.py:310
  88.6 3.2 fusion
  98.3 25.2 %all-gather.32.cloned.1.call-done = bf16[4096,128]{0,1:T(8,128)(2,1)} async-done(((bf16[1024,128]{0,1:T(8,128)(2,1)}), bf16[4096,128]{0,1:T(8,128)(2,1)}) %all-gather.32.cloned.1.call-update) | async-done | bytes 1048592 | tf_op jit(solution)/shard_map/all_gather | solution.py:310
  126.7 22.2 %attend.1 = (bf16[1024,256]{1,0:T(8,128)(2,1)}, f32[1024,256]{1,0:T(8,128)}, f32[8,4,128]{2,1,0:T(4,128)}) custom-call(s32[16]{0:T(128)} %doc_ref.3, s32[1]{0:T(128)} %bitcast.at_ref, bf16[1024,256]{1,0:T(8,128)(2,1)} %copy.73.q_ref, bf16[4096,128]{1,0:T(8,128)(2,1)} %bitcast.134), custom_call_target="tpu_custom_call" | custom-call | flops 1073741824 | bytes 8388608 | tf_op jit(solution)/shard_map/attend/pallas_call | solution.py:166
  149.5 3.1 all-gather.18.cloned.1.call-done
  152.6 39.2 %all-gather.16.cloned.1.call-done = bf16[1024,2048]{1,0:T(8,128)(2,1)} async-done(((bf16[1024,256]{1,0:T(8,128)(2,1)}), bf16[1024,2048]{1,0:T(8,128)(2,1)}) %all-gather.16.cloned.1.call-update) | async-done | bytes 4194320 | tf_op jit(solution)/shard_map/all_gather | solution.py:310
  191.7 4.6 convolution_convert_fusion.8
  196.3 3.6 all-to-all-start
  200.1 15.2 %all-to-all-done = bf16[8,128,256]{2,1,0:T(8,128)(2,1)S(1)} async-done(((bf16[8,128,256]{2,1,0:T(8,128)(2,1)}), bf16[8,128,256]{2,1,0:T(8,128)(2,1)S(1)}, u32[]{:S(2)}, u32[]{:S(2)}) %all-to-all-start) | async-done | bytes 524320 | tf_op jit(solution)/shard_map/all_to_all | solution.py:385
  219.1 13.7 %all-gather.22.cloned.1.call-done = bf16[1024,2048]{1,0:T(8,128)(2,1)} async-done(((bf16[256,2048]{1,0:T(8,128)(2,1)}), bf16[1024,2048]{1,0:T(8,128)(2,1)}) %all-gather.22.cloned.1.call-update) | async-done | bytes 4194320 | tf_op jit(solution)/shard_map/all_gather | solution.py:310
  232.8 76.1 %all-gather.20.cloned.1.call-done = bf16[1024,2048]{1,0:T(8,128)(2,1)} async-done(((bf16[128,2048]{1,0:T(8,128)(2,1)}), bf16[1024,2048]{1,0:T(8,128)(2,1)}) %all-gather.20.cloned.1.call-update) | async-done | bytes 4194320 | tf_op jit(solution)/shard_map/all_gather | solution.py:310
  308.9 10.0 fusion.55
  318.9 24.3 %all-gather.24.cloned.1.call-done = bf16[1024,2048]{1,0:T(8,128)(2,1)} async-done(((bf16[256,2048]{1,0:T(8,128)(2,1)}), bf16[1024,2048]{1,0:T(8,128)(2,1)}) %all-gather.24.cloned.1.call-update) | async-done | bytes 4194320 | tf_op jit(solution)/shard_map/all_gather | solution.py:310
  343.2 10.0 fusion.56
  353.3 26.0 %all-gather.26.cloned.1.call-done = bf16[1024,2048]{1,0:T(8,128)(2,1)} async-done(((bf16[256,2048]{1,0:T(8,128)(2,1)}), bf16[1024,2048]{1,0:T(8,128)(2,1)}) %all-gather.26.cloned.1.call-update) | async-done | bytes 4194320 | tf_op jit(solution)/shard_map/all_gather | solution.py:310
  379.3 75.4 %all-gather.28.cloned.1.call-done = bf16[1024,2048]{1,0:T(8,128)(2,1)} async-done(((bf16[128,2048]{1,0:T(8,128)(2,1)}), bf16[1024,2048]{1,0:T(8,128)(2,1)}) %all-gather.28.cloned.1.call-update) | async-done | bytes 4194320 | tf_op jit(solution)/shard_map/all_gather | solution.py:310
  454.8 13.3 %multiply_convert_fusion = (bf16[1024,1024]{1,0:T(8,128)(2,1)S(1)}, bf16[1024,1024]{1,0:T(8,128)(2,1)S(1)}, bf16[1024,1024]{1,0:T(8,128)(2,1)}) fusion(f32[1024,1024]{1,0:T(8,128)} %fusion.55, f32[1024,1024]{1,0:T(8,128)} %fusion.56, bf16[1024,2048]{1,0:T(8,128)(2,1)} %all-gather.28.cloned.1.call-done, bf16[1024,2048]{1,0:T(8,128)(2,1)} %all-gather.26.cloned.1.call-done), kind=kOutput, calls=%fused_computation.6 | convolution fusion | flops 4310695936 | bytes 23068672 | tf_op jit(solution)/shard_map/dot_general | solution.py:35
  468.1 7.2 fusion.57
  475.3 8.3 add_convert_fusion
  483.6 86.2 %reduce-scatter.13.cloned.1.call-done = bf16[128,2048]{1,0:T(8,128)(2,1)} async-done(((bf16[1024,2048]{1,0:T(8,128)(2,1)}), bf16[128,2048]{1,0:T(8,128)(2,1)}) %reduce-scatter.13.cloned.1.call-update) | async-done | bytes 524304 | tf_op jit(solution)/shard_map/reduce_scatter | solution.py:314
  572.8 13.2 %all_to_all.32 = bf16[128,8,256]{2,0,1:T(8,128)(2,1)S(1)} all-to-all(bf16[128,8,256]{2,0,1:T(8,128)(2,1)S(1)} %bitcast.128), channel_id=1, replica_groups=mesh['y'=2,'x'=2,'c'=2,'r'=1,'z'=4] {'y','x','c'}, dimensions={1} | all-to-all | bytes 1048576 | tf_op jit(solution)/shard_map/all_to_all | solution.py:415
  586.0 3.2 convolution_convert_fusion.1
  589.3 49.4 %reduce-scatter.15.cloned.1.call-done.do_ref = bf16[1024,256]{1,0:T(8,128)(2,1)} async-done(((bf16[1024,2048]{1,0:T(8,128)(2,1)}), bf16[1024,256]{1,0:T(8,128)(2,1)}) %reduce-scatter.15.cloned.1.call-update) | async-done | bytes 524304 | tf_op jit(solution)/shard_map/reduce_scatter | solution.py:314
  638.7 24.4 %attend_back.1 = (f32[1024,256]{1,0:T(8,128)}, bf16[4096,128]{1,0:T(8,128)(2,1)}) custom-call(s32[16]{0:T(128)} %doc_ref.3, s32[1]{0:T(128)} %bitcast.at_ref, bf16[1024,256]{1,0:T(8,128)(2,1)} %copy.73.q_ref, bf16[1024,256]{1,0:T(8,128)(2,1)} %reduce-scatter.15.cloned.1.call-done.do_ref, f32[1024,256]{1,0:T(8,128)} %get-tuple-element.18.of_ref, ...), custom_call_target="tpu_custom_call" | custom-call | flops 2684354560 | bytes 12582912 | tf_op jit(solution)/shard_map/attend_back/pallas_call | solution.py:279
  665.8 2.7 copy.89
  668.7 9.4 convolution_convert_fusion.4
  678.1 9.5 convolution_convert_fusion.3
  687.9 9.5 convolution_convert_fusion.2
  697.5 4.5 convolution_convert_fusion.7
  702.1 2.8 copy.77
  711.2 4.5 convolution_convert_fusion.6
  717.6 4.4 convolution_convert_fusion
  723.6 8.2 convolution_convert_fusion.5
  732.4 6.5 reduce-scatter.25.cloned.1.call-done
  738.9 2.8 convert_element_type.138
  741.7 44.2 %reduce-scatter.27.cloned.1.call-done = bf16[256,2048]{1,0:T(8,128)(2,1)} async-done(((bf16[1024,2048]{1,0:T(8,128)(2,1)}), bf16[256,2048]{1,0:T(8,128)(2,1)}) %reduce-scatter.27.cloned.1.call-update) | async-done | bytes 1048592 | tf_op jit(solution)/shard_map/reduce_scatter | solution.py:314
  785.8 2.8 convert_element_type.140
  788.6 44.3 %reduce-scatter.29.cloned.1.call-done = bf16[256,2048]{1,0:T(8,128)(2,1)} async-done(((bf16[1024,2048]{1,0:T(8,128)(2,1)}), bf16[256,2048]{1,0:T(8,128)(2,1)}) %reduce-scatter.29.cloned.1.call-update) | async-done | bytes 1048592 | tf_op jit(solution)/shard_map/reduce_scatter | solution.py:314
  832.9 2.8 convert_element_type.142
  835.7 26.6 %reduce-scatter.23.cloned.1.call-done = bf16[64,2048]{1,0:T(8,128)(2,1)} async-done(((bf16[256,2048]{1,0:T(8,128)(2,1)}), bf16[64,2048]{1,0:T(8,128)(2,1)}) %reduce-scatter.23.cloned.1.call-update) | async-done | bytes 262160 | tf_op jit(solution)/shard_map/reduce_scatter | solution.py:314
  868.4 2.7 copy.81
  873.8 2.8 fusion.5
  876.8 21.7 %reduce-scatter.21.cloned.1.call-done = bf16[1,96,2048]{2,1,0:T(8,128)(2,1)} async-done(((bf16[4,96,2048]{2,1,0:T(8,128)(2,1)}), bf16[1,96,2048]{2,1,0:T(8,128)(2,1)}) %reduce-scatter.21.cloned.1.call-update) | async-done | bytes 393232 | tf_op jit(solution)/shard_map/reduce_scatter | solution.py:314
  901.1 51.4 %reduce-scatter.19.cloned.1.call-done = bf16[128,2048]{1,0:T(8,128)(2,1)} async-done(((bf16[1024,2048]{1,0:T(8,128)(2,1)}), bf16[128,2048]{1,0:T(8,128)(2,1)}) %reduce-scatter.19.cloned.1.call-update) | async-done | bytes 524304 | tf_op jit(solution)/shard_map/reduce_scatter | solution.py:314
  954.3 42.0 %all-reduce.1 = f32[32,132]{1,0:T(8,128)S(1)} all-reduce(f32[32,132]{1,0:T(8,128)S(1)} %maximum_maximum_fusion), channel_id=10, replica_groups=mesh['y'=2,'x'=2,'c'=2,'r'=1,'z'=4] {'y','x','c','r','z'}, use_global_device_ids=true, to_apply=%region_19.20.clone | all-reduce | flops 4224 | bytes 33792
  997.4 47.8 %reduce-scatter.11.cloned.1.call-done = bf16[128,2048]{1,0:T(8,128)(2,1)} async-done(((bf16[1024,2048]{1,0:T(8,128)(2,1)}), bf16[128,2048]{1,0:T(8,128)(2,1)}) %reduce-scatter.11.cloned.1.call-update) | async-done | bytes 524304 | tf_op jit(solution)/shard_map/reduce_scatter | solution.py:314
  1045.2 3.0 fusion.13
  (169 shorter events, 52.8 us)
Async XLA Ops:
  7.2 49.4 %all-gather.30.cloned.1.call-start = ((), (), s32[]{:S(2)}) async-start(), calls=%async_computation.30 | async-start | bytes 1966080 | tf_op jit(solution)/shard_map/all_gather | solution.py:310
  9.0 79.5 %all-gather.14.cloned.1.call-start = ((), (), s32[]{:S(2)}) async-start(), calls=%async_computation.12 | async-start | bytes 4718592 | tf_op jit(solution)/shard_map/all_gather | solution.py:310
  9.8 113.7 %all-gather.32.cloned.1.call-start = ((), (), s32[]{:S(2)}) async-start(), calls=%async_computation.31 | async-start | bytes 1310720 | tf_op jit(solution)/shard_map/all_gather | solution.py:310
  57.9 36.0 %copy-start.8 = (bf16[4,64,2048]{2,1,0:T(8,128)(2,1)}, bf16[4,64,2048]{2,1,0:T(8,128)(2,1)S(1)}, u32[]{:S(2)}) copy-start(bf16[4,64,2048]{2,1,0:T(8,128)(2,1)S(1)} %slice.147) | copy-start | bytes 3145732
  59.4 34.5 %copy-start.11 = (bf16[4,16,2048]{2,1,0:T(8,128)(2,1)}, bf16[4,16,2048]{2,1,0:T(8,128)(2,1)S(1)}, u32[]{:S(2)}) copy-start(bf16[4,16,2048]{2,1,0:T(8,128)(2,1)S(1)} %get-tuple-element.37) | copy-start | bytes 786436
  59.4 34.5 %copy-start.13 = (bf16[4,16,2048]{2,1,0:T(8,128)(2,1)}, bf16[4,16,2048]{2,1,0:T(8,128)(2,1)S(1)}, u32[]{:S(2)}) copy-start(bf16[4,16,2048]{2,1,0:T(8,128)(2,1)S(1)} %get-tuple-element.38) | copy-start | bytes 786436
  88.5 3.4 copy-start.7
  95.4 57.1 %all-gather.18.cloned.1.call-start = ((), (), s32[]{:S(2)}) async-start(), calls=%async_computation.14 | async-start | bytes 1310720 | tf_op jit(solution)/shard_map/all_gather | solution.py:310
  96.0 95.7 %all-gather.16.cloned.1.call-start = ((), (), s32[]{:S(2)}) async-start(), calls=%async_computation.13 | async-start | bytes 4718592 | tf_op jit(solution)/shard_map/all_gather | solution.py:310
  148.9 83.8 %all-gather.22.cloned.1.call-start = ((), (), s32[]{:S(2)}) async-start(), calls=%async_computation.16 | async-start | bytes 5242880 | tf_op jit(solution)/shard_map/all_gather | solution.py:310
  196.3 19.1 %copy-start = (bf16[128,2048]{1,0:T(8,128)(2,1)S(1)}, bf16[128,2048]{1,0:T(8,128)(2,1)}, u32[]{:S(2)}) copy-start(bf16[128,2048]{1,0:T(8,128)(2,1)} %param.13) | copy-start | bytes 1572868
  196.3 18.9 %all-to-all-start = ((bf16[8,128,256]{2,1,0:T(8,128)(2,1)}), bf16[8,128,256]{2,1,0:T(8,128)(2,1)S(1)}, u32[]{:S(2)}, u32[]{:S(2)}) async-start(bf16[8,128,256]{2,1,0:T(8,128)(2,1)} %bitcast.12), calls=%async_computation | async-start | bytes 1048576 | tf_op jit(solution)/shard_map/all_to_all | solution.py:385
  199.9 109.0 %all-gather.20.cloned.1.call-start = ((), (), s32[]{:S(2)}) async-start(), calls=%async_computation.15 | async-start | bytes 4718592 | tf_op jit(solution)/shard_map/all_gather | solution.py:310
  216.7 126.5 %all-gather.24.cloned.1.call-start = ((), (), s32[]{:S(2)}) async-start(), calls=%async_computation.17 | async-start | bytes 5242880 | tf_op jit(solution)/shard_map/all_gather | solution.py:310
  217.5 161.9 %all-gather.26.cloned.1.call-start = ((), (), s32[]{:S(2)}) async-start(), calls=%async_computation.18 | async-start | bytes 5242880 | tf_op jit(solution)/shard_map/all_gather | solution.py:310
  218.2 236.5 %all-gather.28.cloned.1.call-start = ((), (), s32[]{:S(2)}) async-start(), calls=%async_computation.20 | async-start | bytes 4718592 | tf_op jit(solution)/shard_map/all_gather | solution.py:310
  218.8 351.1 %reduce-scatter.13.cloned.1.call-start = ((), (), s32[]{:S(2)}) async-start(), calls=%async_computation.21 | async-start | bytes 4718592 | tf_op jit(solution)/shard_map/reduce_scatter | solution.py:314
  454.8 13.3 %copy-start.19 = (bf16[1024,2048]{1,0:T(8,128)(2,1)S(1)}, bf16[1024,2048]{1,0:T(8,128)(2,1)}, u32[]{:S(2)}) copy-start(bf16[1024,2048]{1,0:T(8,128)(2,1)} %all-gather.22.cloned.1.call-done) | copy-start | bytes 12582916
  468.0 7.2 copy-start.23
  468.0 7.2 copy-start.22
  468.1 7.2 copy-start.20
  483.6 87.8 %copy-start.2 = (bf16[128,2048]{1,0:T(8,128)(2,1)S(1)}, bf16[128,2048]{1,0:T(8,128)(2,1)}, u32[]{:S(2)}) copy-start(bf16[128,2048]{1,0:T(8,128)(2,1)} %param.25) | copy-start | bytes 1572868
  483.6 155.1 %reduce-scatter.15.cloned.1.call-start = ((), (), s32[]{:S(2)}) async-start(), calls=%async_computation.22 | async-start | bytes 4718592 | tf_op jit(solution)/shard_map/reduce_scatter | solution.py:314
  569.9 16.1 %copy-start.10 = (bf16[256,2048]{1,0:T(8,128)(2,1)S(1)}, bf16[256,2048]{1,0:T(8,128)(2,1)}, u32[]{:S(2)}) copy-start(bf16[256,2048]{1,0:T(8,128)(2,1)} %all-gather.18.cloned.1.call-done) | copy-start | bytes 3145732
  589.3 119.4 %reduce-scatter.17.cloned.1.call-start = ((), (), s32[]{:S(2)}) async-start(), calls=%async_computation.23 | async-start | bytes 1310720 | tf_op jit(solution)/shard_map/reduce_scatter | solution.py:314
  668.5 70.4 %reduce-scatter.25.cloned.1.call-start = ((), (), s32[]{:S(2)}) async-start(), calls=%async_computation.27 | async-start | bytes 5242880 | tf_op jit(solution)/shard_map/reduce_scatter | solution.py:314
  678.1 107.8 %reduce-scatter.27.cloned.1.call-start = ((), (), s32[]{:S(2)}) async-start(), calls=%async_computation.28 | async-start | bytes 5242880 | tf_op jit(solution)/shard_map/reduce_scatter | solution.py:314
  687.6 145.3 %reduce-scatter.29.cloned.1.call-start = ((), (), s32[]{:S(2)}) async-start(), calls=%async_computation.29 | async-start | bytes 5242880 | tf_op jit(solution)/shard_map/reduce_scatter | solution.py:314
  697.4 164.9 %reduce-scatter.23.cloned.1.call-start = ((), (), s32[]{:S(2)}) async-start(), calls=%async_computation.26 | async-start | bytes 1310720 | tf_op jit(solution)/shard_map/reduce_scatter | solution.py:314
  702.0 196.5 %reduce-scatter.21.cloned.1.call-start = ((), (), s32[]{:S(2)}) async-start(), calls=%async_computation.25 | async-start | bytes 1966080 | tf_op jit(solution)/shard_map/reduce_scatter | solution.py:314
  706.3 0.8 copy-start.5
  706.3 1.1 copy-start.6
  709.7 0.9 copy-start.15
  710.5 0.7 copy-start.17
  715.6 1.6 copy-start.9
  715.7 1.6 copy-start.12
  715.7 1.7 copy-start.14
  715.7 1.8 copy-start.16
  715.7 1.9 copy-start.18
  717.2 235.4 %reduce-scatter.19.cloned.1.call-start = ((), (), s32[]{:S(2)}) async-start(), calls=%async_computation.24 | async-start | bytes 4718592 | tf_op jit(solution)/shard_map/reduce_scatter | solution.py:314
  722.0 1.6 copy-start.21
  722.0 323.2 %reduce-scatter.11.cloned.1.call-start = ((), (), s32[]{:S(2)}) async-start(), calls=%async_computation.19 | async-start | bytes 4718592 | tf_op jit(solution)/shard_map/reduce_scatter | solution.py:314
  876.6 168.6 %copy-start.1 = (bf16[128,2048]{1,0:T(8,128)(2,1)S(1)}, bf16[128,2048]{1,0:T(8,128)(2,1)}, u32[]{:S(2)}) copy-start(bf16[128,2048]{1,0:T(8,128)(2,1)} %param.13) | copy-start | bytes 1572868
  876.6 168.6 %copy-start.3 = (bf16[128,2048]{1,0:T(8,128)(2,1)S(1)}, bf16[128,2048]{1,0:T(8,128)(2,1)}, u32[]{:S(2)}) copy-start(bf16[128,2048]{1,0:T(8,128)(2,1)} %param.25) | copy-start | bytes 1572868
  876.7 168.6 %copy-start.4 = (bf16[128,2048]{1,0:T(8,128)(2,1)S(1)}, bf16[128,2048]{1,0:T(8,128)(2,1)}, u32[]{:S(2)}) copy-start(bf16[128,2048]{1,0:T(8,128)(2,1)} %reduce-scatter.13.cloned.1.call-done) | copy-start | bytes 1572868
Sparse Core Ops, SparseCore 0:
  10.2 40.8 all-gather.29
  52.9 35.5 all-gather.13
  95.6 27.9 all-gather.31
  124.9 27.5 all-gather.17
  154.9 36.8 all-gather.15
  193.1 39.5 all-gather.21
  235.5 73.4 all-gather.19
  310.5 32.7 all-gather.23
  344.8 34.4 all-gather.25
  381.3 73.4 all-gather.27
  483.7 86.1 reduce-scatter.12
  589.4 49.2 reduce-scatter.14
  668.6 24.4 reduce-scatter.16
  695.7 43.1 reduce-scatter.24
  741.3 44.5 reduce-scatter.26
  788.4 44.5 reduce-scatter.28
  835.1 27.1 reduce-scatter.22
  864.5 33.9 reduce-scatter.20
  902.2 50.2 reduce-scatter.18
  956.0 89.1 reduce-scatter.10
